TPU v7x, 128 devices: a whole 4x4x4 slice. The times are simulated.
128 devices in a mesh: pts: 8 (over x, core), shk: 16 (over z, y).
Axes of the slice: x: 4, y: 4, z: 4, core: 2. Of those that a mesh axis runs over, the one named last changes fastest.
Arguments:
- savings: float32 [16, 59, 1024], P('shk', None, 'pts'), may hold values from 0.05 to 0.95
- wealth: float32 [16, 59, 1024], P('shk', None, 'pts'), may hold values from 0.5 to 2
- surplus: bfloat16 [16, 118, 2048], P('shk', None, 'pts'), may hold values from -0.12 to 0.12
- point_dims: int32 [16, 3, 2048], P('shk', None, 'pts'), may hold values from 0 to 58
- point_levels: int32 [16, 3, 2048], P('shk', None, 'pts'), may hold values from 0 to 3
- point_index: int32 [16, 3, 2048], P('shk', None, 'pts'), may hold values from 1 to 7, as said below
- live_count: int32 [16, 8], P('shk', 'pts'), may hold values from 64 to 256
- trans_counts: int32 [16, 16], replicated, may hold values from 1 to 99
Outputs:
- savings_out: float32 [16, 59, 1024], P('shk', None, 'pts')
- consumption: float32 [16, 59, 1024], P('shk', None, 'pts')
Inputs may be any that keep to these rules, and one draw needn't show every extreme that they name: `point_index`: odd, below 2 ** level where the level is positive, 1 where it is 0. Points at positions from live_count on in a shard are padding.
All inputs are finite; a program needn't handle non-finite values.
Results may differ from a plain program's by a relative error of at most 0.0011.
Values may be sent and summed in bfloat16 or wider, within the bound.
No kernel may reach another device: no remote copies, remote signals or barrier semaphores. Data moves between devices by JAX's collectives and lax.ppermute only.
A program may use at most 192 MiB of HBM per device.

v0:
```python
import jax
import jax.numpy as jnp
from jax import lax
from jax.sharding import PartitionSpec as P

ITERS = 2
GAMMA = 2.0
BETA = 0.96
damping = 0.5
query_block = 2048


def hat_tables(levels, indices):
    scaled = jnp.exp2(levels.astype(jnp.float32))
    inverse = jnp.where(levels > 0, scaled, jnp.zeros_like(scaled))
    centre = indices.astype(jnp.float32) / scaled
    return (centre, inverse)


def basis_block(coords, dims, centre, inverse):
    chosen = jnp.take(coords, dims, axis=0)
    factor = jnp.maximum(0.0, 1.0 - jnp.abs(chosen - centre[:, :, None]) * inverse[:, :, None])
    product = factor[0]
    for slot in range(1, factor.shape[0]):
        product = product * factor[slot]
    return product.astype(jnp.bfloat16)


def make_evaluate(weights, dims, centre, inverse):

    def block_eval(coords):
        basis = basis_block(coords, dims, centre, inverse)
        return jnp.dot(weights, basis, preferred_element_type=jnp.float32)

    def evaluate(piece, start):
        coords = piece.astype(jnp.float32)
        breadth = coords.shape[1]
        stacked = coords.reshape(coords.shape[0], breadth // query_block, query_block).transpose(
            1, 0, 2
        )
        results = lax.map(block_eval, stacked)
        return results.transpose(1, 0, 2).reshape(results.shape[1], breadth)

    return evaluate


def per_device(
    savings, wealth, surplus, point_dims, point_levels, point_index, live_count, trans_counts
):
    npoints = surplus.shape[2]
    live = live_count[0, 0]
    position = lax.iota(jnp.int32, npoints)
    live_surplus = jnp.where(position[None, :] < live, surplus[0], jnp.zeros_like(surplus[0]))
    counts = trans_counts.astype(jnp.float32)
    prob = counts / jnp.sum(counts, axis=1, keepdims=True)
    shock = lax.axis_index("shk")
    shk_count = lax.axis_size("shk")
    current = savings[0]
    income = wealth[0]
    dimension = current.shape[0]
    nquery = current.shape[1]
    centre, inverse = hat_tables(point_levels[0], point_index[0])
    evaluate = make_evaluate(live_surplus, point_dims[0], centre, inverse)
    consumption = current
    for sweep in range(ITERS):
        query = current.astype(jnp.bfloat16)
        partial_value = evaluate(
            lax.all_gather(query, ("pts", "shk"), axis=1, tiled=True), jnp.int32(0)
        )
        mine = lax.psum_scatter(partial_value, "pts", scatter_dimension=1, tiled=True)
        marginal = jnp.exp(-GAMMA * mine[:dimension] + mine[dimension:]).reshape(
            dimension, shk_count, nquery
        )
        column = lax.dynamic_index_in_dim(prob, shock, 1, keepdims=False)
        terms = marginal * column[None, :, None]
        expect = lax.psum_scatter(terms, "shk", scatter_dimension=1, tiled=True)[:, 0, :]
        consumption = (BETA * expect) ** (-1.0 / GAMMA)
        current = (1.0 - damping) * current + damping * jax.nn.sigmoid(income - consumption)
    return (current[None], consumption[None])


def solution(mesh):
    return jax.shard_map(
        per_device,
        mesh=mesh,
        in_specs=(
            P("shk", None, "pts"),
            P("shk", None, "pts"),
            P("shk", None, "pts"),
            P("shk", None, "pts"),
            P("shk", None, "pts"),
            P("shk", None, "pts"),
            P("shk", "pts"),
            P(),
        ),
        out_specs=(P("shk", None, "pts"), P("shk", None, "pts")),
        check_vma=False,
    )
```

profile of v0, /device:TPU:0, one launch (start us, length us, event | category | flops | bytes accessed | tf_op | source)
XLA Modules:
  0.0 647.1 jit_solution(12382082039239027195)
XLA Ops:
  11.5 66.2 %all-gather.3.cloned.1.call-done = bf16[59,16384]{1,0:T(8,128)(2,1)} async-done(((bf16[59,128]{1,0:T(8,128)(2,1)}), bf16[59,16384]{1,0:T(8,128)(2,1)}) %all-gather.3.cloned.1.call-update) | async-done | bytes 1933328 | tf_op jit(solution)/shard_map/all_gather | solution.py:68
  82.6 4.2 copy.73
  86.8 4.0 broadcast.101.clone
  90.8 90.0 %while.20 = (s32[]{:T(128)}, f32[8,118,2048]{2,1,0:T(8,128)}, f32[8,59,2048]{2,1,0:T(8,128)}, s32[3,256]{1,0:T(4,128)S(1)}, f32[3,256]{1,0:T(4,128)S(1)}, /*inde...) while((s32[]{:T(128)}, f32[8,118,2048]{2,1,0:T(8,128)}, f32[8,59,2048]{2,1,0:T(8,128)}, ...), condition=%wide.region_1.3_spmd, body=%wide.region_0.0_spmd.sunk | while | flops 134749952 | bytes 33501272 | solution.py:41
  91.9 5.0 gather_fusion
  97.0 3.6 fusion.49
  103.1 5.0 gather_fusion
  108.1 3.6 fusion.49
  114.3 5.0 gather_fusion
  119.4 3.6 fusion.49
  125.5 5.0 gather_fusion
  130.6 3.6 fusion.49
  136.7 5.0 gather_fusion
  141.7 3.6 fusion.49
  147.9 5.0 gather_fusion
  152.9 3.6 fusion.49
  159.1 5.0 gather_fusion
  164.1 3.6 fusion.49
  170.3 5.0 gather_fusion
  175.3 3.6 fusion.49
  180.8 7.7 %copy.26 = f32[118,8,2048]{2,1,0:T(8,128)S(1)} copy(f32[118,8,2048]{2,0,1:T(8,128)} %bitcast.15) | data formatting | bytes 15466496 | tf_op jit(solution)/shard_map/transpose | solution.py:42
  189.5 9.0 %copy.40 = f32[15,8,8,2048]{3,1,2,0:T(8,128)} copy(f32[15,8,8,2048]{3,2,1,0:T(8,128)S(1)} %bitcast.133) | data formatting | bytes 15728640
  199.5 48.4 %reduce-scatter.9.cloned.1.call-done = f32[118,2048]{1,0:T(8,128)} async-done(((f32[118,16384]{1,0:T(8,128)}), f32[118,2048]{1,0:T(8,128)}) %reduce-scatter.9.cloned.1.call-update) | async-done | bytes 966672 | tf_op jit(solution)/shard_map/reduce_scatter | solution.py:70
  250.5 74.0 %reduce-scatter.13.cloned.1.call-done = f32[59,1,128]{2,0,1:T(8,128)} async-done(((f32[59,16,128]{2,0,1:T(8,128)}), f32[59,1,128]{2,0,1:T(8,128)}) %reduce-scatter.13.cloned.1.call-update) | async-done | bytes 30224
  325.9 64.9 %all-gather.5.cloned.1.call-done = bf16[59,16384]{1,0:T(8,128)(2,1)} async-done(((bf16[59,128]{1,0:T(8,128)(2,1)}), bf16[59,16384]{1,0:T(8,128)(2,1)}) %all-gather.5.cloned.1.call-update) | async-done | bytes 1933328 | tf_op jit(solution)/shard_map/all_gather | solution.py:68
  395.6 4.2 copy.72
  399.8 4.0 broadcast.101
  403.9 89.7 %while.21 = (s32[]{:T(128)}, f32[8,118,2048]{2,1,0:T(8,128)}, f32[8,59,2048]{2,1,0:T(8,128)}, s32[3,256]{1,0:T(4,128)S(1)}, f32[3,256]{1,0:T(4,128)S(1)}, /*inde...) while((s32[]{:T(128)}, f32[8,118,2048]{2,1,0:T(8,128)}, f32[8,59,2048]{2,1,0:T(8,128)}, ...), condition=%wide.region_6.8_spmd, body=%wide.region_5.7_spmd.sunk | while | flops 134749952 | bytes 33501272 | solution.py:41
  405.0 5.0 gather_fusion.1
  410.0 3.6 fusion.53
  416.1 5.0 gather_fusion.1
  421.2 3.6 fusion.53
  427.4 5.0 gather_fusion.1
  432.4 3.6 fusion.53
  438.6 5.0 gather_fusion.1
  443.6 3.6 fusion.53
  449.8 5.0 gather_fusion.1
  454.8 3.6 fusion.53
  460.9 5.0 gather_fusion.1
  466.0 3.6 fusion.53
  472.1 5.0 gather_fusion.1
  477.2 3.6 fusion.53
  483.3 5.0 gather_fusion.1
  488.4 3.6 fusion.53
  493.6 7.7 %copy.31 = f32[118,8,2048]{2,1,0:T(8,128)S(1)} copy(f32[118,8,2048]{2,0,1:T(8,128)} %bitcast.19) | data formatting | bytes 15466496 | tf_op jit(solution)/shard_map/transpose | solution.py:42
  502.3 9.0 %copy.43 = f32[15,8,8,2048]{3,1,2,0:T(8,128)} copy(f32[15,8,8,2048]{3,2,1,0:T(8,128)S(1)} %bitcast.132) | data formatting | bytes 15728640
  511.4 49.4 %reduce-scatter.11.cloned.1.call-done = f32[118,2048]{1,0:T(8,128)} async-done(((f32[118,16384]{1,0:T(8,128)}), f32[118,2048]{1,0:T(8,128)}) %reduce-scatter.11.cloned.1.call-update) | async-done | bytes 966672 | tf_op jit(solution)/shard_map/reduce_scatter | solution.py:70
  563.2 73.9 %reduce-scatter.15.cloned.1.call-done = f32[59,1,128]{2,0,1:T(8,128)} async-done(((f32[59,16,128]{2,0,1:T(8,128)}), f32[59,1,128]{2,0,1:T(8,128)}) %reduce-scatter.15.cloned.1.call-update) | async-done | bytes 30224
  (145 shorter events, 66.0 us)
Async XLA Ops:
  7.2 70.6 %all-gather.3.cloned.1.call-start = ((), (), s32[]{:S(2)}) async-start(), calls=%async_computation.4 | async-start | bytes 2113536 | tf_op jit(solution)/shard_map/all_gather | solution.py:68
  8.6 239.4 %reduce-scatter.9.cloned.1.call-start = ((), (), s32[]{:S(2)}) async-start(), calls=%async_computation.5 | async-start | bytes 8847360 | tf_op jit(solution)/shard_map/reduce_scatter | solution.py:70
  198.5 0.7 copy-start.3
  198.5 125.9 %copy-start = (f32[1,59,128]{2,0,1:T(1,128)S(1)}, f32[1,59,128]{2,0,1:T(1,128)}, u32[]{:S(2)}) copy-start(f32[1,59,128]{2,0,1:T(1,128)} %param.14) | copy-start | bytes 90628
  198.5 125.9 %copy-start.2 = (f32[1,59,128]{2,0,1:T(1,128)S(1)}, f32[1,59,128]{2,0,1:T(1,128)}, u32[]{:S(2)}) copy-start(f32[1,59,128]{2,0,1:T(1,128)} %param.15) | copy-start | bytes 90628
  198.5 125.9 %reduce-scatter.13.cloned.1.call-start = ((), (), s32[]{:S(2)}) async-start(), calls=%async_computation.8 | async-start | bytes 557056
  250.4 140.4 %all-gather.5.cloned.1.call-start = ((), (), s32[]{:S(2)}) async-start(), calls=%async_computation.6 | async-start | bytes 2113536 | tf_op jit(solution)/shard_map/all_gather | solution.py:68
  325.9 234.9 %reduce-scatter.11.cloned.1.call-start = ((), (), s32[]{:S(2)}) async-start(), calls=%async_computation.7 | async-start | bytes 8847360 | tf_op jit(solution)/shard_map/reduce_scatter | solution.py:70
  511.3 125.9 %copy-start.1 = (f32[59,1,128]{2,0,1:T(8,128)S(1)}, f32[59,1,128]{2,0,1:T(8,128)}, u32[]{:S(2)}) copy-start(f32[59,1,128]{2,0,1:T(8,128)} %reduce-scatter.13.cloned.1.call-done) | copy-start | bytes 90628
  511.3 125.8 %reduce-scatter.15.cloned.1.call-start = ((), (), s32[]{:S(2)}) async-start(), calls=%async_computation.9 | async-start | bytes 557056
Sparse Core Ops, SparseCore 0:
  11.3 66.3 all-gather.2
  198.7 49.2 reduce-scatter.8
  251.1 73.2 reduce-scatter.12
  327.7 63.0 all-gather.4
  511.5 49.2 reduce-scatter.10
  563.8 73.3 reduce-scatter.14
where the time goes:
time: 655 us; the launch traced here: 647 us
  waiting for transfers between devices  377 us (58%)
  local copies, waits for them, and re-layouts  160 us (24%)
  other arithmetic  71.1 us (11%)
  matrix products  22.8 us (3%)
  between operations  15.1 us (2%)
    unnamed x8, waiting for transfers between devices  148 us
    all_gather x2, waiting for transfers between devices, per_device(): lax.all_gather(query, ('pts', 'shk'), axis=1, tiled=True)  131 us
    reduce_scatter x2, waiting for transfers between devices, per_device(): lax.psum_scatter(partial_value, 'pts', scatter_dimension=1, tiled=True)  97.8 us
    gather x16, local copies, waits for them, and re-layouts, basis_block(): chosen = jnp.take(coords, dims, axis=0)  80.3 us
    max x16, other arithmetic, basis_block(): jnp.maximum(0.0, 1.0 - jnp.abs(chosen - centre[:, :, None]) * inverse[:,...  57.7 us
    unnamed x20, local copies, waits for them, and re-layouts  29 us
    dot_general x16, matrix products, block_eval(): return jnp.dot(weights, basis, preferred_element_type=jnp.float32)  22.8 us
    squeeze x16, local copies, waits for them, and re-layouts, evaluate(): results = lax.map(block_eval, stacked)  17.2 us
  transfers between devices with their start and end apart: 6, of which 6 were waited for; matrix products, arithmetic and copies ran while one was open for 0% of the time, Pallas kernels for 0%

commit v1 on v0

--- a/solution.py
+++ b/solution.py
@@ -65,7 +65,13 @@
     for sweep in range(ITERS):
         query = current.astype(jnp.bfloat16)
         partial_value = evaluate(
-            lax.all_gather(query, ("pts", "shk"), axis=1, tiled=True), jnp.int32(0)
+            jnp.concatenate(
+                lax.all_to_all(
+                    jnp.stack([query] * lax.axis_size(("pts", "shk"))), ("pts", "shk"), 0, 0
+                ),
+                axis=1,
+            ),
+            jnp.int32(0),
         )
         mine = lax.psum_scatter(partial_value, "pts", scatter_dimension=1, tiled=True)
         marginal = jnp.exp(-GAMMA * mine[:dimension] + mine[dimension:]).reshape(

time: 655 us -> 618 us (0.944)
  waiting for transfers between devices: 377 us -> 268 us
  blocking collectives: 0 us -> 37.5 us
  local copies, waits for them, and re-layouts: 160 us -> 189 us
  starting transfers between devices: 0.42 us -> 11.5 us
    all_gather x2 -> x0, waiting for transfers between devices: 131 us -> none  [per_device(): lax.all_gather(query, ('pts', 'shk'), axis=1, tiled=True)]
    dynamic_slice x0 -> x32, local copies, waits for them, and re-layouts: none -> 42.4 us  [evaluate(): results = lax.map(block_eval, stacked)]
    all_to_all x0 -> x1, blocking collectives: none -> 37.5 us  [per_device(): lax.all_to_all(jnp.stack([query] * lax.axis_size(('pts', 'shk'))), ('pts'...]
    all_to_all x0 -> x1, waiting for transfers between devices: none -> 29 us  [per_device(): lax.all_to_all(jnp.stack([query] * lax.axis_size(('pts', 'shk'))), ('pts'...]
    squeeze x16 -> x0, local copies, waits for them, and re-layouts: 17.2 us -> none  [evaluate(): results = lax.map(block_eval, stacked)]
    all_to_all x0 -> x1, starting transfers between devices: none -> 11.2 us  [per_device(): lax.all_to_all(jnp.stack([query] * lax.axis_size(('pts', 'shk'))), ('pts'...]
    transpose x4, local copies, waits for them, and re-layouts: 9.3 us -> 17.7 us  [evaluate(): coords.reshape(coords.shape[0], breadth // query_block, query_block)]
    unnamed x20 -> x26, local copies, waits for them, and re-layouts: 29 us -> 22 us
  transfers between devices with their start and end apart: 6 -> 5, of which waited for: 6 -> 5; matrix products, arithmetic and copies ran while one was open for 0% -> 0% of each run, Pallas kernels for 0% -> 0%
where the time goes in v1:
time: 618 us; the launch traced here: 611 us
  waiting for transfers between devices  268 us (43%)
  local copies, waits for them, and re-layouts  189 us (31%)
  other arithmetic  67 us (11%)
  blocking collectives  37.5 us (6%)
  matrix products  23 us (4%)
  between operations  14.9 us (2%)
  starting transfers between devices  11.5 us (2%)
    unnamed x6, waiting for transfers between devices  148 us
    reduce_scatter x2, waiting for transfers between devices, per_device(): lax.psum_scatter(partial_value, 'pts', scatter_dimension=1, tiled=True)  90.8 us
    gather x16, local copies, waits for them, and re-layouts, basis_block(): chosen = jnp.take(coords, dims, axis=0)  80.3 us
    max x16, other arithmetic, basis_block(): jnp.maximum(0.0, 1.0 - jnp.abs(chosen - centre[:, :, None]) * inverse[:,...  57.7 us
    dynamic_slice x32, local copies, waits for them, and re-layouts, evaluate(): results = lax.map(block_eval, stacked)  42.4 us
    all_to_all x1, blocking collectives, per_device(): lax.all_to_all(jnp.stack([query] * lax.axis_size(('pts', 'shk'))), ('pts'...  37.5 us
    all_to_all x1, waiting for transfers between devices, per_device(): lax.all_to_all(jnp.stack([query] * lax.axis_size(('pts', 'shk'))), ('pts'...  29 us
    dot_general x16, matrix products, block_eval(): return jnp.dot(weights, basis, preferred_element_type=jnp.float32)  23 us
  transfers between devices with their start and end apart: 5, of which 5 were waited for; matrix products, arithmetic and copies ran while one was open for 0% of the time, Pallas kernels for 0%

profile of v1, /device:TPU:0, one launch (start us, length us, event | category | flops | bytes accessed | tf_op | source)
XLA Modules:
  0.0 611.4 jit_solution(8692054768825686446)
XLA Ops:
  9.9 11.2 %all-to-all-start = ((bf16[128,59,128]{2,1,0:T(8,128)(2,1)}), bf16[128,59,128]{2,1,0:T(8,128)(2,1)S(1)}, u32[]{:S(2)}, u32[]{:S(2)}) async-start(bf16[128,59,128]{2,1,0:T(8,128)(2,1)} %stack.9), calls=%async_computation | async-start | bytes 4194304 | tf_op jit(solution)/shard_map/all_to_all | solution.py:69
  21.9 29.0 %all-to-all-done = bf16[128,59,128]{2,1,0:T(8,128)(2,1)S(1)} async-done(((bf16[128,59,128]{2,1,0:T(8,128)(2,1)}), bf16[128,59,128]{2,1,0:T(8,128)(2,1)S(1)}, u32[]{:S(2)}, u32[]{:S(2)}) %all-to-all-start) | async-done | bytes 1933344 | tf_op jit(solution)/shard_map/all_to_all | solution.py:69
  51.3 4.1 copy.20
  55.4 4.8 reshape.103
  60.2 4.0 broadcast.100.clone
  64.2 102.7 %while.20 = (s32[]{:T(128)}, f32[8,118,2048]{2,1,0:T(8,128)}, f32[8,59,2048]{2,0,1:T(8,128)}, s32[3,256]{1,0:T(4,128)S(1)}, f32[3,256]{1,0:T(4,128)S(1)}, /*inde...) while((s32[]{:T(128)}, f32[8,118,2048]{2,1,0:T(8,128)}, f32[8,59,2048]{2,0,1:T(8,128)}, ...), condition=%wide.region_1.3_spmd, body=%wide.region_0.0_spmd.sunk | while | flops 134749952 | bytes 34467928 | solution.py:41
  66.9 5.0 gather_fusion
  72.0 3.6 fusion.41
  79.7 5.0 gather_fusion
  84.7 3.6 fusion.41
  92.5 5.0 gather_fusion
  97.6 3.6 fusion.41
  105.3 5.0 gather_fusion
  110.3 3.6 fusion.41
  118.1 5.0 gather_fusion
  123.1 3.6 fusion.41
  130.9 5.0 gather_fusion
  135.9 3.6 fusion.41
  143.6 5.0 gather_fusion
  148.7 3.6 fusion.41
  156.4 5.0 gather_fusion
  161.5 3.6 fusion.41
  166.9 7.7 %copy.25 = f32[118,8,2048]{2,1,0:T(8,128)S(1)} copy(f32[118,8,2048]{2,0,1:T(8,128)} %bitcast.113) | data formatting | bytes 15466496 | tf_op jit(solution)/shard_map/transpose | solution.py:42
  175.7 9.0 %copy.40 = f32[15,8,8,2048]{3,1,2,0:T(8,128)} copy(f32[15,8,8,2048]{3,2,1,0:T(8,128)S(1)} %bitcast.110) | data formatting | bytes 15728640
  185.7 44.9 %reduce-scatter.9.cloned.1.call-done = f32[118,2048]{1,0:T(8,128)} async-done(((f32[118,16384]{1,0:T(8,128)}), f32[118,2048]{1,0:T(8,128)}) %reduce-scatter.9.cloned.1.call-update) | async-done | bytes 966672 | tf_op jit(solution)/shard_map/reduce_scatter | solution.py:76
  233.1 74.0 %reduce-scatter.13.cloned.1.call-done = f32[59,1,128]{2,0,1:T(8,128)} async-done(((f32[59,16,128]{2,0,1:T(8,128)}), f32[59,1,128]{2,0,1:T(8,128)}) %reduce-scatter.13.cloned.1.call-update) | async-done | bytes 30224
  308.4 37.5 %all_to_all.10 = bf16[128,59,128]{2,1,0:T(8,128)(2,1)S(1)} all-to-all(bf16[128,59,128]{2,1,0:T(8,128)(2,1)S(1)} %stack.11), channel_id=1, replica_groups=mesh['pts'=8,'shk'=16] {'pts','shk'}, dimensions={0} | all-to-all | bytes 3866624 | tf_op jit(solution)/shard_map/all_to_all | solution.py:69
  346.4 4.1 copy.29
  350.5 4.8 reshape.104
  355.3 4.0 broadcast.100
  359.3 102.4 %while.21 = (s32[]{:T(128)}, f32[8,118,2048]{2,1,0:T(8,128)}, f32[8,59,2048]{2,0,1:T(8,128)}, s32[3,256]{1,0:T(4,128)S(1)}, f32[3,256]{1,0:T(4,128)S(1)}, /*inde...) while((s32[]{:T(128)}, f32[8,118,2048]{2,1,0:T(8,128)}, f32[8,59,2048]{2,0,1:T(8,128)}, ...), condition=%wide.region_6.8_spmd, body=%wide.region_5.7_spmd.sunk | while | flops 134749952 | bytes 34467928 | solution.py:41
  362.0 5.0 gather_fusion.1
  367.0 3.6 fusion.45
  374.8 5.0 gather_fusion.1
  379.8 3.6 fusion.45
  387.6 5.0 gather_fusion.1
  392.6 3.6 fusion.45
  400.4 5.0 gather_fusion.1
  405.4 3.6 fusion.45
  413.2 5.0 gather_fusion.1
  418.2 3.6 fusion.45
  425.9 5.0 gather_fusion.1
  438.7 5.0 gather_fusion.1
  451.5 5.0 gather_fusion.1
  461.8 7.7 %copy.31 = f32[118,8,2048]{2,1,0:T(8,128)S(1)} copy(f32[118,8,2048]{2,0,1:T(8,128)} %bitcast.114) | data formatting | bytes 15466496 | tf_op jit(solution)/shard_map/transpose | solution.py:42
  470.5 9.0 %copy.42 = f32[15,8,8,2048]{3,1,2,0:T(8,128)} copy(f32[15,8,8,2048]{3,2,1,0:T(8,128)S(1)} %bitcast.109) | data formatting | bytes 15728640
  479.6 45.8 %reduce-scatter.11.cloned.1.call-done = f32[118,2048]{1,0:T(8,128)} async-done(((f32[118,16384]{1,0:T(8,128)}), f32[118,2048]{1,0:T(8,128)}) %reduce-scatter.11.cloned.1.call-update) | async-done | bytes 966672 | tf_op jit(solution)/shard_map/reduce_scatter | solution.py:76
  527.9 73.9 %reduce-scatter.15.cloned.1.call-done = f32[59,1,128]{2,0,1:T(8,128)} async-done(((f32[59,16,128]{2,0,1:T(8,128)}), f32[59,1,128]{2,0,1:T(8,128)}) %reduce-scatter.15.cloned.1.call-update) | async-done | bytes 30224
  (167 shorter events, 92.4 us)
Async XLA Ops:
  7.2 14.6 %copy-start.5 = (s32[1,3,256]{2,0,1:T(1,128)S(1)}, s32[1,3,256]{2,0,1:T(1,128)}, u32[]{:S(2)}) copy-start(s32[1,3,256]{2,0,1:T(1,128)} %param.17) | copy-start | bytes 9220
  7.2 14.6 %copy-start.6 = (s32[1,3,256]{2,0,1:T(1,128)S(1)}, s32[1,3,256]{2,0,1:T(1,128)}, u32[]{:S(2)}) copy-start(s32[1,3,256]{2,0,1:T(1,128)} %param.18) | copy-start | bytes 9220
  7.2 14.6 %copy-start.7 = (s32[1,3,256]{2,0,1:T(1,128)S(1)}, s32[1,3,256]{2,0,1:T(1,128)}, u32[]{:S(2)}) copy-start(s32[1,3,256]{2,0,1:T(1,128)} %param.19) | copy-start | bytes 9220
  7.2 14.7 %copy-start.3 = (bf16[1,118,256]{2,1,0:T(8,128)(2,1)S(1)}, bf16[1,118,256]{2,1,0:T(8,128)(2,1)}, u32[]{:S(2)}) copy-start(bf16[1,118,256]{2,1,0:T(8,128)(2,1)} %param.16) | copy-start | bytes 181252
  9.9 41.0 %all-to-all-start = ((bf16[128,59,128]{2,1,0:T(8,128)(2,1)}), bf16[128,59,128]{2,1,0:T(8,128)(2,1)S(1)}, u32[]{:S(2)}, u32[]{:S(2)}) async-start(bf16[128,59,128]{2,1,0:T(8,128)(2,1)} %stack.9), calls=%async_computation | async-start | bytes 4194304 | tf_op jit(solution)/shard_map/all_to_all | solution.py:69
  21.1 209.5 %reduce-scatter.9.cloned.1.call-start = ((), (), s32[]{:S(2)}) async-start(), calls=%async_computation.6 | async-start | bytes 8847360 | tf_op jit(solution)/shard_map/reduce_scatter | solution.py:76
  184.7 0.7 copy-start.4
  184.7 122.4 %copy-start = (f32[1,59,128]{2,0,1:T(1,128)S(1)}, f32[1,59,128]{2,0,1:T(1,128)}, u32[]{:S(2)}) copy-start(f32[1,59,128]{2,0,1:T(1,128)} %param.14) | copy-start | bytes 90628
  184.7 122.4 %copy-start.2 = (f32[1,59,128]{2,0,1:T(1,128)S(1)}, f32[1,59,128]{2,0,1:T(1,128)}, u32[]{:S(2)}) copy-start(f32[1,59,128]{2,0,1:T(1,128)} %param.15) | copy-start | bytes 90628
  184.7 122.4 %reduce-scatter.13.cloned.1.call-start = ((), (), s32[]{:S(2)}) async-start(), calls=%async_computation.8 | async-start | bytes 557056
  233.1 292.4 %reduce-scatter.11.cloned.1.call-start = ((), (), s32[]{:S(2)}) async-start(), calls=%async_computation.7 | async-start | bytes 8847360 | tf_op jit(solution)/shard_map/reduce_scatter | solution.py:76
  479.5 122.3 %copy-start.1 = (f32[59,1,128]{2,0,1:T(8,128)S(1)}, f32[59,1,128]{2,0,1:T(8,128)}, u32[]{:S(2)}) copy-start(f32[59,1,128]{2,0,1:T(8,128)} %reduce-scatter.13.cloned.1.call-done) | copy-start | bytes 90628
  479.5 122.3 %reduce-scatter.15.cloned.1.call-start = ((), (), s32[]{:S(2)}) async-start(), calls=%async_computation.9 | async-start | bytes 557056
Sparse Core Ops, SparseCore 0:
  184.8 45.7 reduce-scatter.8
  233.8 73.2 reduce-scatter.12
  479.6 45.7 reduce-scatter.10
  528.4 73.3 reduce-scatter.14
